TPU v7x, 32 devices: a whole 2x2x4 slice. The times are simulated.
32 devices in a mesh: expert: 8 (over z, core), dp: 4 (over y, x).
Axes of the slice: x: 2, y: 2, z: 4, core: 2. Of those that a mesh axis runs over, the one named last changes fastest.
Arguments:
- tokens: bfloat16 [4096, 1024], P(('expert', 'dp')), may hold values from -6 to 6
- out_grad: bfloat16 [4096, 1024], P(('expert', 'dp')), may hold values from -0.59765625 to 0.59765625
- expert_ids: int32 [4096, 3], P(('expert', 'dp')), may hold values from 0 to 7, all different within a row; in each aligned block of 128 rows (0 to 127, 128 to 255, ...) at most 64 rows name the same one
- gate_probs: float32 [4096, 3], P(('expert', 'dp')), may hold values from 0.05 to 0.5
- w_gate: bfloat16 [8, 1024, 384], P('expert'), may hold values from -0.1875 to 0.1875
- w_up: bfloat16 [8, 1024, 384], P('expert'), may hold values from -0.1875 to 0.1875
- w_down: bfloat16 [8, 384, 1024], P('expert'), may hold values from -0.3125 to 0.3125
Outputs:
- grad_gate: bfloat16 [8, 1024, 384], P('expert', 'dp')
- grad_up: bfloat16 [8, 1024, 384], P('expert', 'dp')
- grad_down: bfloat16 [8, 384, 1024], P('expert', 'dp')
Inputs may be any that keep to these rules, and one draw needn't show every extreme that they name: `expert_ids`: each row names 3 different experts. In the 128 rows of one device no expert is named by more than 64 rows, a bound that some block reaches.
All inputs are finite; a program needn't handle non-finite values.
Results may differ from a plain program's by a relative error of at most 0.018.
Values may be sent and summed in bfloat16 or wider, within the bound.
A program may use at most 64 MiB of HBM per device.

v0:
```python
import jax
import jax.numpy as jnp
from jax import lax
from jax.sharding import PartitionSpec as P


def contract_rows(left, right):
    return lax.dot_general(
        left, right, (((0,), (0,)), ((), ())), preferred_element_type=jnp.float32
    )


def shards(tokens, out_grad, expert_ids, gate_probs, w_gate, w_up, w_down):
    experts = lax.axis_size("expert")
    tok_rows = tokens.shape[0]
    top_k = expert_ids.shape[1]
    width = tokens.shape[1]
    capacity = min(tok_rows, 4 * tok_rows * top_k // (3 * experts))
    columns = jnp.arange(experts, dtype=jnp.int32)
    hits = (expert_ids[:, :, None] == columns).astype(jnp.int32)
    token_hits = jnp.sum(hits, axis=1)
    before = jnp.cumsum(token_hits, axis=0) - token_hits
    rank = jnp.sum(hits * before[:, None, :], axis=2)
    scaled = (gate_probs[:, :, None] * out_grad[:, None, :].astype(jnp.float32)).astype(
        jnp.bfloat16
    )
    repeated = jnp.broadcast_to(tokens[:, None, :], scaled.shape)
    flat_slot = (expert_ids * capacity + rank).reshape(-1)
    send_in = (
        jnp.zeros((experts * capacity, width), jnp.bfloat16)
        .at[flat_slot]
        .set(repeated.reshape(-1, width))
    )
    send_grad = (
        jnp.zeros((experts * capacity, width), jnp.bfloat16)
        .at[flat_slot]
        .set(scaled.reshape(-1, width))
    )
    send_in = send_in.reshape(experts, capacity, width)
    send_grad = send_grad.reshape(experts, capacity, width)
    got_in, got_grad = (
        lax.all_to_all(send_in, "expert", split_axis=0, concat_axis=0, tiled=True),
        lax.all_to_all(send_grad, "expert", split_axis=0, concat_axis=0, tiled=True),
    )
    rows_in = got_in.reshape(-1, width)
    rows_grad = got_grad.reshape(-1, width)
    gate_pre = jnp.dot(rows_in, w_gate[0], preferred_element_type=jnp.float32)
    up_pre = jnp.dot(rows_in, w_up[0], preferred_element_type=jnp.float32)
    sigma = jax.nn.sigmoid(gate_pre)
    active = gate_pre * sigma
    hidden = (active * up_pre).astype(jnp.bfloat16)
    grad_down = contract_rows(hidden, rows_grad)
    grad_hidden = lax.dot_general(
        rows_grad, w_down[0], (((1,), (1,)), ((), ())), preferred_element_type=jnp.float32
    )
    grad_upper = (grad_hidden * active).astype(jnp.bfloat16)
    grad_gate_pre = (grad_hidden * up_pre * sigma * (1.0 + gate_pre * (1.0 - sigma))).astype(
        jnp.bfloat16
    )
    grad_gate = contract_rows(rows_in, grad_gate_pre)
    grad_up = contract_rows(rows_in, grad_upper)
    sum_gate, sum_up, sum_down = (
        lax.psum_scatter(
            grad_gate[None].astype(jnp.bfloat16), "dp", scatter_dimension=1, tiled=True
        ).astype(jnp.float32),
        lax.psum_scatter(
            grad_up[None].astype(jnp.bfloat16), "dp", scatter_dimension=1, tiled=True
        ).astype(jnp.float32),
        lax.psum_scatter(
            grad_down[None].astype(jnp.bfloat16), "dp", scatter_dimension=1, tiled=True
        ).astype(jnp.float32),
    )
    return (
        sum_gate.astype(jnp.bfloat16),
        sum_up.astype(jnp.bfloat16),
        sum_down.astype(jnp.bfloat16),
    )


def solution(mesh):
    return jax.shard_map(
        shards,
        mesh=mesh,
        in_specs=(
            P(("expert", "dp"), None),
            P(("expert", "dp"), None),
            P(("expert", "dp"), None),
            P(("expert", "dp"), None),
            P("expert", None, None),
            P("expert", None, None),
            P("expert", None, None),
        ),
        out_specs=(P("expert", "dp", None), P("expert", "dp", None), P("expert", "dp", None)),
        check_vma=False,
    )
```

profile of v0, /device:TPU:0, one launch (start us, length us, event | category | flops | bytes accessed | tf_op | source)
XLA Modules:
  0.0 173.8 jit_solution(15862193931348732459)
XLA Ops:
  7.2 0.0 copy-start
  7.2 0.8 convert_reduce_fusion
  7.9 0.1 copy.14
  8.0 0.2 reduce_window_sum.11
  8.3 0.7 select_reduce_fusion
  9.0 0.7 multiply_add_fusion
  9.7 0.1 copy.17
  9.8 0.2 reshape.73
  10.0 1.3 broadcast_in_dim.2
  11.3 0.7 reshape.83
  12.0 0.0 copy-start.5
  12.0 3.1 %scatter_custom_fusion = bf16[512,1024]{1,0:T(8,128)(2,1)} fusion(s32[384]{0:T(512)S(1)} %fusion.18, bf16[384,1024]{1,0:T(8,128)(2,1)S(1)} %reshape.83, bf16[]{:T(256)} %constant.5.clone.1), kind=kCustom, calls=%fused_computation.23 | custom fusion | bytes 1048578 | tf_op jit(solution)/shard_map/scatter | solution.py:32
  15.1 6.4 %all-to-all-start = ((bf16[8,64,1024]{2,1,0:T(8,128)(2,1)}), bf16[8,64,1024]{2,1,0:T(8,128)(2,1)S(1)}, u32[]{:S(2)}, u32[]{:S(2)}) async-start(bf16[8,64,1024]{2,1,0:T(8,128)(2,1)} %bitcast), calls=%async_computation | async-start | bytes 2097152 | tf_op jit(solution)/shard_map/all_to_all | solution.py:42
  21.5 0.0 copy-done.5
  21.5 1.9 %mul.59 = f32[128,3,1024]{2,1,0:T(4,128)} broadcast(bf16[128,1024]{1,0:T(8,128)(2,1)S(1)} %copy-done.5), dimensions={0,2} | broadcast | bytes 1835008 | tf_op jit(solution)/shard_map/mul | solution.py:24
  23.4 0.0 copy-start.6
  23.4 2.7 %mul.60 = f32[384,1024]{1,0:T(8,128)S(1)} reshape(f32[128,3,1024]{2,1,0:T(4,128)} %mul.59) | data formatting | bytes 3145728 | tf_op jit(solution)/shard_map/mul | solution.py:24
  26.1 0.0 copy-done.6
  26.1 0.1 copy.18
  26.2 0.2 mul.57
  26.5 3.1 %scatter_custom_fusion.1 = bf16[512,1024]{1,0:T(8,128)(2,1)} fusion(s32[384]{0:T(512)S(1)} %fusion.18, f32[384,1024]{1,0:T(8,128)S(1)} %mul.60, f32[384]{0:T(512)S(1)} %mul.57, bf16[]{:T(256)} %constant.5.clone.1), kind=kCustom, calls=%fused_computation.9 | custom fusion | flops 786432 | bytes 2623490 | tf_op jit(solution)/shard_map/scatter | solution.py:37
  29.6 18.4 %all-to-all-done = bf16[8,64,1024]{2,1,0:T(8,128)(2,1)S(1)} async-done(((bf16[8,64,1024]{2,1,0:T(8,128)(2,1)}), bf16[8,64,1024]{2,1,0:T(8,128)(2,1)S(1)}, u32[]{:S(2)}, u32[]{:S(2)}) %all-to-all-start) | async-done | bytes 1048608 | tf_op jit(solution)/shard_map/all_to_all | solution.py:42
  48.0 3.6 %all-to-all-start.1 = ((bf16[8,64,1024]{2,1,0:T(8,128)(2,1)}), bf16[8,64,1024]{2,1,0:T(8,128)(2,1)S(1)}, u32[]{:S(2)}, u32[]{:S(2)}) async-start(bf16[8,64,1024]{2,1,0:T(8,128)(2,1)} %bitcast.31), calls=%async_computation.1 | async-start | bytes 2097152 | tf_op jit(solution)/shard_map/all_to_all | solution.py:43
  51.6 0.0 reduce-scatter.4.cloned.1.call-start
  51.7 0.0 copy-start.1
  51.7 0.0 copy-done
  51.7 1.6 fusion.4
  53.3 0.0 copy-done.1
  53.3 1.6 fusion.6
  54.9 23.2 %all-to-all-done.1 = bf16[8,64,1024]{2,1,0:T(8,128)(2,1)S(1)} async-done(((bf16[8,64,1024]{2,1,0:T(8,128)(2,1)}), bf16[8,64,1024]{2,1,0:T(8,128)(2,1)S(1)}, u32[]{:S(2)}, u32[]{:S(2)}) %all-to-all-start.1) | async-done | bytes 1048608 | tf_op jit(solution)/shard_map/all_to_all | solution.py:43
  78.1 0.0 copy-start.2
  78.1 0.0 copy-start.3
  78.1 2.0 %fusion.8 = f32[512,384]{1,0:T(8,128)S(1)} fusion(bf16[512,1024]{1,0:T(8,128)(2,1)S(1)} %bitcast.29, bf16[1,384,1024]{2,1,0:T(8,128)(2,1)} %param.13), kind=kOutput, calls=%fused_computation.14 | convolution fusion | flops 402653184 | bytes 2621440 | tf_op jit(solution)/shard_map/dot_general | solution.py:53
  80.1 0.0 copy-start.4
  80.1 0.9 copy-done.4
  81.0 0.0 copy-done.2
  81.0 0.0 copy-done.3
  81.0 1.8 %fusion = bf16[1,1024,384]{2,1,0:T(8,128)(2,1)} fusion(bf16[512,1024]{1,0:T(8,128)(2,1)S(1)} %bitcast.27, f32[512,384]{1,0:T(8,128)S(1)} %copy-done.2, f32[512,384]{1,0:T(8,128)S(1)} %fusion.8, f32[512,384]{1,0:T(8,128)S(1)} %copy-done.3), kind=kOutput, calls=%fused_computation.6 | convolution fusion | flops 405012480 | bytes 4194304 | tf_op jit(solution)/shard_map/dot_general | solution.py:8
  82.7 0.0 reduce-scatter.4.cloned.1.call-update
  82.8 0.0 reduce-scatter.6.cloned.1.call-start
  82.8 3.1 %fusion.1 = bf16[1,1024,384]{2,1,0:T(8,128)(2,1)} fusion(bf16[512,1024]{1,0:T(8,128)(2,1)S(1)} %bitcast.28, f32[512,384]{1,0:T(8,128)} %copy-done.4, f32[512,384]{1,0:T(8,128)} %fusion.4), kind=kOutput, calls=%fused_computation.7 | convolution fusion | flops 404226048 | bytes 3407872 | tf_op jit(solution)/shard_map/dot_general | solution.py:8
  85.9 0.0 reduce-scatter.6.cloned.1.call-update
  85.9 0.0 reduce-scatter.8.cloned.1.call-start
  86.0 2.9 %fusion.2 = bf16[1,384,1024]{2,1,0:T(8,128)(2,1)} fusion(bf16[512,1024]{1,0:T(8,128)(2,1)S(1)} %bitcast.30, f32[512,384]{1,0:T(8,128)} %fusion.6, f32[512,384]{1,0:T(8,128)} %fusion.4), kind=kOutput, calls=%fused_computation.8 | convolution fusion | flops 404226048 | bytes 3407872 | tf_op jit(solution)/shard_map/dot_general | solution.py:8
  88.9 0.0 reduce-scatter.8.cloned.1.call-update
  88.9 19.1 %reduce-scatter.4.cloned.1.call-done = bf16[1,256,384]{2,1,0:T(8,128)(2,1)} async-done(((bf16[1,1024,384]{2,1,0:T(8,128)(2,1)}), bf16[1,256,384]{2,1,0:T(8,128)(2,1)}) %reduce-scatter.4.cloned.1.call-update) | async-done | bytes 196624 | tf_op jit(solution)/shard_map/reduce_scatter | solution.py:63
  108.0 29.7 %reduce-scatter.6.cloned.1.call-done = bf16[1,256,384]{2,1,0:T(8,128)(2,1)} async-done(((bf16[1,1024,384]{2,1,0:T(8,128)(2,1)}), bf16[1,256,384]{2,1,0:T(8,128)(2,1)}) %reduce-scatter.6.cloned.1.call-update) | async-done | bytes 196624 | tf_op jit(solution)/shard_map/reduce_scatter | solution.py:66
  137.6 29.7 %reduce-scatter.8.cloned.1.call-done = bf16[1,96,1024]{2,1,0:T(8,128)(2,1)} async-done(((bf16[1,384,1024]{2,1,0:T(8,128)(2,1)}), bf16[1,96,1024]{2,1,0:T(8,128)(2,1)}) %reduce-scatter.8.cloned.1.call-update) | async-done | bytes 196624 | tf_op jit(solution)/shard_map/reduce_scatter | solution.py:69
  (3 shorter events, 0.1 us)
Async XLA Ops:
  7.2 44.5 %copy-start = (bf16[1,1024,384]{2,1,0:T(8,128)(2,1)S(1)}, bf16[1,1024,384]{2,1,0:T(8,128)(2,1)}, u32[]{:S(2)}) copy-start(bf16[1,1024,384]{2,1,0:T(8,128)(2,1)} %param.11) | copy-start | bytes 2359300
  12.0 9.5 %copy-start.5 = (bf16[128,1024]{1,0:T(8,128)(2,1)S(1)}, bf16[128,1024]{1,0:T(8,128)(2,1)}, u32[]{:S(2)}) copy-start(bf16[128,1024]{1,0:T(8,128)(2,1)} %param.8) | copy-start | bytes 786436
  15.1 32.9 %all-to-all-start = ((bf16[8,64,1024]{2,1,0:T(8,128)(2,1)}), bf16[8,64,1024]{2,1,0:T(8,128)(2,1)S(1)}, u32[]{:S(2)}, u32[]{:S(2)}) async-start(bf16[8,64,1024]{2,1,0:T(8,128)(2,1)} %bitcast), calls=%async_computation | async-start | bytes 2097152 | tf_op jit(solution)/shard_map/all_to_all | solution.py:42
  23.4 2.7 %copy-start.6 = (f32[128,3]{0,1:T(4,128)S(1)}, f32[128,3]{0,1:T(4,128)}, u32[]{:S(2)}) copy-start(f32[128,3]{0,1:T(4,128)} %param.10) | copy-start | bytes 4612
  48.0 30.1 %all-to-all-start.1 = ((bf16[8,64,1024]{2,1,0:T(8,128)(2,1)}), bf16[8,64,1024]{2,1,0:T(8,128)(2,1)S(1)}, u32[]{:S(2)}, u32[]{:S(2)}) async-start(bf16[8,64,1024]{2,1,0:T(8,128)(2,1)} %bitcast.31), calls=%async_computation.1 | async-start | bytes 2097152 | tf_op jit(solution)/shard_map/all_to_all | solution.py:43
  51.6 56.4 %reduce-scatter.4.cloned.1.call-start = ((), (), s32[]{:S(2)}) async-start(), calls=%async_computation.5 | async-start | bytes 983040 | tf_op jit(solution)/shard_map/reduce_scatter | solution.py:63
  51.7 1.6 copy-start.1
  78.1 2.9 %copy-start.2 = (f32[512,384]{1,0:T(8,128)S(1)}, f32[512,384]{1,0:T(8,128)}, u32[]{:S(2)}) copy-start(f32[512,384]{1,0:T(8,128)} %fusion.4) | copy-start | bytes 2359300
  78.1 2.9 %copy-start.3 = (f32[512,384]{1,0:T(8,128)S(1)}, f32[512,384]{1,0:T(8,128)}, u32[]{:S(2)}) copy-start(f32[512,384]{1,0:T(8,128)} %fusion.6) | copy-start | bytes 2359300
  80.1 0.9 copy-start.4
  82.8 54.9 %reduce-scatter.6.cloned.1.call-start = ((), (), s32[]{:S(2)}) async-start(), calls=%async_computation.6 | async-start | bytes 983040 | tf_op jit(solution)/shard_map/reduce_scatter | solution.py:66
  85.9 81.4 %reduce-scatter.8.cloned.1.call-start = ((), (), s32[]{:S(2)}) async-start(), calls=%async_computation.7 | async-start | bytes 983040 | tf_op jit(solution)/shard_map/reduce_scatter | solution.py:69
Sparse Core Ops, SparseCore 0:
  82.9 25.0 reduce-scatter.3
  111.5 26.1 reduce-scatter.5
  141.1 26.1 reduce-scatter.7
where the time goes:
time: 174 us
  waiting for transfers between devices  120 us (69%)
  between operations  13.8 us (8%)
  matrix products  12.9 us (7%)
  local copies, waits for them, and re-layouts  11.4 us (7%)
  starting transfers between devices  10 us (6%)
  other arithmetic  5.52 us (3%)
    reduce_scatter x1, waiting for transfers between devices, shards(): lax.psum_scatter(grad_down[None].astype(jnp.bfloat16), 'dp', scatter_dime...  29.7 us
    reduce_scatter x1, waiting for transfers between devices, shards(): lax.psum_scatter(grad_up[None].astype(jnp.bfloat16), 'dp', scatter_dimens...  29.7 us
    all_to_all x1, waiting for transfers between devices, shards(): lax.all_to_all(send_grad, 'expert', split_axis=0, concat_axis=0, tiled=True)  23.2 us
    reduce_scatter x1, waiting for transfers between devices, shards(): lax.psum_scatter(grad_gate[None].astype(jnp.bfloat16), 'dp', scatter_dime...  19.1 us
    all_to_all x1, waiting for transfers between devices, shards(): lax.all_to_all(send_in, 'expert', split_axis=0, concat_axis=0, tiled=True)  18.4 us
    dot_general x3, matrix products, contract_rows(): lax.dot_general(left, right, (((0,), (0,)), ((), ())), preferred_element_...  7.74 us
    all_to_all x1, starting transfers between devices, shards(): lax.all_to_all(send_in, 'expert', split_axis=0, concat_axis=0, tiled=True)  6.35 us
    mul x3, local copies, waits for them, and re-layouts, shards(): gate_probs[:, :, None] * out_grad[:, None, :].astype(jnp.float32)  4.83 us
  transfers between devices with their start and end apart: 5, of which 5 were waited for; matrix products, arithmetic and copies ran while one was open for 10% of the time, Pallas kernels for 0%

commit v1 on v0

--- a/solution.py
+++ b/solution.py
@@ -1,7 +1,27 @@
+import functools
 import jax
 import jax.numpy as jnp
 from jax import lax
 from jax.sharding import PartitionSpec as P
+
+
+def fix_the_arrays(arr, a_name):
+    prior, mid_arr = (lax.axis_size(a_name), lax.axis_index(a_name))
+    tmp = arr.shape[0] // prior
+    lower = list(arr.shape)
+    lower[0] = tmp
+    back = lower[0]
+    lower[0] = back * prior
+    newest = jnp.zeros(lower, arr.dtype)
+    for j in range(prior):
+        clean = lax.dynamic_slice_in_dim(arr, (mid_arr ^ j) * tmp, tmp, axis=0)
+        if j:
+            clean = lax.ppermute(clean, a_name, list(map(lambda rr: (rr, rr ^ j), range(prior))))
+        newest = lax.dynamic_update_slice_in_dim(newest, clean, (mid_arr ^ j) * back, axis=0)
+    return newest
+
+
+make_figure = functools.partial(fix_the_arrays, a_name="expert")
 
 
 def contract_rows(left, right):
@@ -40,7 +60,7 @@
     send_grad = send_grad.reshape(experts, capacity, width)
     got_in, got_grad = (
         lax.all_to_all(send_in, "expert", split_axis=0, concat_axis=0, tiled=True),
-        lax.all_to_all(send_grad, "expert", split_axis=0, concat_axis=0, tiled=True),
+        make_figure(send_grad),
     )
     rows_in = got_in.reshape(-1, width)
     rows_grad = got_grad.reshape(-1, width)

time: 174 us -> 165 us (0.948)
  waiting for transfers between devices: 120 us -> 105 us
  starting transfers between devices: 10 us -> 17.2 us
  matrix products: 12.9 us -> 9.46 us
  local copies, waits for them, and re-layouts: 11.4 us -> 14 us
    all_to_all x1 -> x0, waiting for transfers between devices: 23.2 us -> none  [shards(): lax.all_to_all(send_grad, 'expert', split_axis=0, concat_axis=0, tiled=True)]
    ppermute x0 -> x7, waiting for transfers between devices: none -> 22.5 us  [fix_the_arrays(): lax.ppermute(clean, a_name, list(map(lambda rr: (rr, rr ^ j), range(prior...]
    all_to_all x1, waiting for transfers between devices: 18.4 us -> 0.01 us  [shards(): lax.all_to_all(send_in, 'expert', split_axis=0, concat_axis=0, tiled=True)]
    ppermute x0 -> x7, starting transfers between devices: none -> 10.8 us  [fix_the_arrays(): lax.ppermute(clean, a_name, list(map(lambda rr: (rr, rr ^ j), range(prior...]
    reduce_scatter x1, waiting for transfers between devices: 19.1 us -> 29.6 us  [shards(): lax.psum_scatter(grad_gate[None].astype(jnp.bfloat16), 'dp', scatter_dime...]
    reduce_scatter x1, waiting for transfers between devices: 29.7 us -> 22.9 us  [shards(): lax.psum_scatter(grad_down[None].astype(jnp.bfloat16), 'dp', scatter_dime...]
    all_to_all x1 -> x0, starting transfers between devices: 3.56 us -> none  [shards(): lax.all_to_all(send_grad, 'expert', split_axis=0, concat_axis=0, tiled=True)]
    unnamed x15 -> x23, local copies, waits for them, and re-layouts: 1.02 us -> 3.39 us
  transfers between devices with their start and end apart: 5 -> 11, of which waited for: 5 -> 7; matrix products, arithmetic and copies ran while one was open for 10% -> 9% of each run, Pallas kernels for 0% -> 0%
where the time goes in v1:
time: 165 us
  waiting for transfers between devices  105 us (64%)
  starting transfers between devices  17.2 us (10%)
  local copies, waits for them, and re-layouts  14 us (8%)
  between operations  14 us (8%)
  matrix products  9.46 us (6%)
  other arithmetic  5.53 us (3%)
    reduce_scatter x1, waiting for transfers between devices, shards(): lax.psum_scatter(grad_up[None].astype(jnp.bfloat16), 'dp', scatter_dimens...  29.7 us
    reduce_scatter x1, waiting for transfers between devices, shards(): lax.psum_scatter(grad_gate[None].astype(jnp.bfloat16), 'dp', scatter_dime...  29.6 us
    reduce_scatter x1, waiting for transfers between devices, shards(): lax.psum_scatter(grad_down[None].astype(jnp.bfloat16), 'dp', scatter_dime...  22.9 us
    ppermute x7, waiting for transfers between devices, fix_the_arrays(): lax.ppermute(clean, a_name, list(map(lambda rr: (rr, rr ^ j), range(prior...  22.5 us
    ppermute x7, starting transfers between devices, fix_the_arrays(): lax.ppermute(clean, a_name, list(map(lambda rr: (rr, rr ^ j), range(prior...  10.8 us
    all_to_all x1, starting transfers between devices, shards(): lax.all_to_all(send_in, 'expert', split_axis=0, concat_axis=0, tiled=True)  6.35 us
    dot_general x3, matrix products, contract_rows(): lax.dot_general(left, right, (((0,), (0,)), ((), ())), preferred_element_...  6.11 us
    mul x3, local copies, waits for them, and re-layouts, shards(): gate_probs[:, :, None] * out_grad[:, None, :].astype(jnp.float32)  4.82 us
  transfers between devices with their start and end apart: 11, of which 7 were waited for; matrix products, arithmetic and copies ran while one was open for 9% of the time, Pallas kernels for 0%

profile of v1, /device:TPU:0, one launch (start us, length us, event | category | flops | bytes accessed | tf_op | source)
XLA Modules:
  0.0 165.0 jit_solution(293870779955969632)
XLA Ops:
  7.2 0.8 convert_reduce_fusion
  7.9 0.1 copy.14
  8.0 0.2 reduce_window_sum.11
  8.3 0.7 select_reduce_fusion
  9.0 0.7 multiply_add_fusion
  9.7 0.1 copy.17
  9.8 0.2 reshape.73
  10.0 1.3 broadcast_in_dim.4
  11.3 0.7 reshape.83
  12.0 3.1 %scatter_custom_fusion = bf16[512,1024]{1,0:T(8,128)(2,1)} fusion(s32[384]{0:T(512)S(1)} %fusion.18, bf16[384,1024]{1,0:T(8,128)(2,1)S(1)} %reshape.83, bf16[]{:T(256)} %constant.15.clone.1), kind=kCustom, calls=%fused_computation.23 | custom fusion | bytes 1048578 | tf_op jit(solution)/shard_map/scatter | solution.py:52
  15.1 6.4 %all-to-all-start = ((bf16[8,64,1024]{2,1,0:T(8,128)(2,1)}), bf16[8,64,1024]{2,1,0:T(8,128)(2,1)S(1)}, u32[]{:S(2)}, u32[]{:S(2)}) async-start(bf16[8,64,1024]{2,1,0:T(8,128)(2,1)} %bitcast), calls=%async_computation | async-start | bytes 2097152 | tf_op jit(solution)/shard_map/all_to_all | solution.py:62
  21.5 0.0 reduce-scatter.8.cloned.1.call-start
  21.6 1.9 %mul.59 = f32[128,3,1024]{2,1,0:T(4,128)} broadcast(bf16[128,1024]{1,0:T(8,128)(2,1)S(1)} %copy-done.9), dimensions={0,2} | broadcast | bytes 1835008 | tf_op jit(solution)/shard_map/mul | solution.py:44
  23.5 2.7 %mul.60 = f32[384,1024]{1,0:T(8,128)S(1)} reshape(f32[128,3,1024]{2,1,0:T(4,128)} %mul.59) | data formatting | bytes 3145728 | tf_op jit(solution)/shard_map/mul | solution.py:44
  26.2 0.1 copy.18
  26.3 0.2 mul.57
  26.6 3.2 %scatter_custom_fusion.1 = bf16[512,1024]{1,0:T(8,128)(2,1)} fusion(s32[384]{0:T(512)S(1)} %fusion.18, f32[384,1024]{1,0:T(8,128)S(1)} %mul.60, f32[384]{0:T(512)S(1)} %mul.57, bf16[]{:T(256)} %constant.15.clone.1), kind=kCustom, calls=%fused_computation.9 | custom fusion | flops 786432 | bytes 2623490 | tf_op jit(solution)/shard_map/scatter | solution.py:57
  29.7 0.1 broadcast_in_dim.5
  29.8 1.1 copy-done.1
  30.9 0.1 constant_dynamic-slice_fusion
  31.0 0.5 collective-permute-start
  31.5 1.6 collective-permute-start.1
  33.2 2.6 %collective-permute-start.3 = (bf16[1,64,1024]{2,1,0:T(8,128)(2,1)S(1)}, bf16[1,64,1024]{2,1,0:T(8,128)(2,1)S(1)}, u32[]{:S(2)}, u32[]{:S(2)}) collective-permute-start(bf16[1,64,1024]{2,1,0:T(8,128)(2,1)S(1)} %get-tuple-element.6), channel_id=1, source_target_pairs={{0,16},{4,20},{8,24},{12,28},{16,0},{20,4},{24,8},{28,12},{1,17},{... | collective-permute-start | bytes 393224 | tf_op jit(solution)/shard_map/ppermute | solution.py:19
  35.8 0.1 collective-permute-start.4
  35.9 3.4 %collective-permute-start.5 = (bf16[1,64,1024]{2,1,0:T(8,128)(2,1)S(1)}, bf16[1,64,1024]{2,1,0:T(8,128)(2,1)S(1)}, u32[]{:S(2)}, u32[]{:S(2)}) collective-permute-start(bf16[1,64,1024]{2,1,0:T(8,128)(2,1)S(1)} %get-tuple-element.4), channel_id=1, source_target_pairs={{0,24},{4,28},{8,16},{12,20},{16,8},{20,12},{24,0},{28,4},{1,25},{... | collective-permute-start | bytes 393224 | tf_op jit(solution)/shard_map/ppermute | solution.py:19
  39.4 3.1 %collective-permute-done.1 = bf16[1,64,1024]{2,1,0:T(8,128)(2,1)S(1)} collective-permute-done((bf16[1,64,1024]{2,1,0:T(8,128)(2,1)S(1)}, bf16[1,64,1024]{2,1,0:T(8,128)(2,1)S(1)}, u32[]{:S(2)}, u32[]{:S(2)}) %collective-permute-start.1) | collective-permute-done | bytes 131104 | tf_op jit(solution)/shard_map/ppermute | solution.py:19
  42.5 2.4 %collective-permute-start.6 = (bf16[1,64,1024]{2,1,0:T(8,128)(2,1)S(1)}, bf16[1,64,1024]{2,1,0:T(8,128)(2,1)S(1)}, u32[]{:S(2)}, u32[]{:S(2)}) collective-permute-start(bf16[1,64,1024]{2,1,0:T(8,128)(2,1)S(1)} %get-tuple-element.3), channel_id=1, source_target_pairs={{0,28},{4,24},{8,20},{12,16},{16,12},{20,8},{24,4},{28,0},{1,29},{... | collective-permute-start | bytes 393224 | tf_op jit(solution)/shard_map/ppermute | solution.py:19
  44.9 0.3 collective-permute-done.2
  45.3 17.4 %collective-permute-done.3 = bf16[1,64,1024]{2,1,0:T(8,128)(2,1)S(1)} collective-permute-done((bf16[1,64,1024]{2,1,0:T(8,128)(2,1)S(1)}, bf16[1,64,1024]{2,1,0:T(8,128)(2,1)S(1)}, u32[]{:S(2)}, u32[]{:S(2)}) %collective-permute-start.3) | collective-permute-done | bytes 131104 | tf_op jit(solution)/shard_map/ppermute | solution.py:19
  62.7 1.6 collective-permute-done.4
  64.4 0.7 fusion.4
  65.1 0.4 copy-done.2
  65.6 0.7 fusion.6
  66.3 0.2 copy-done.3
  66.4 0.7 copy-done.6
  67.1 1.5 fusion.2
  68.7 0.0 reduce-scatter.8.cloned.1.call-update
  68.7 0.0 reduce-scatter.6.cloned.1.call-start
  68.8 1.9 %fusion.8 = f32[512,384]{1,0:T(8,128)S(1)} fusion(bf16[512,1024]{1,0:T(8,128)(2,1)S(1)} %bitcast.31, bf16[1,384,1024]{2,1,0:T(8,128)(2,1)} %param.13), kind=kOutput, calls=%fused_computation.14 | convolution fusion | flops 402653184 | bytes 2621440 | tf_op jit(solution)/shard_map/dot_general | solution.py:73
  70.7 0.9 copy-done.8
  71.6 1.7 %fusion.1 = bf16[1,1024,384]{2,1,0:T(8,128)(2,1)} fusion(bf16[512,1024]{1,0:T(8,128)(2,1)S(1)} %bitcast.27, f32[512,384]{1,0:T(8,128)S(1)} %fusion.8, f32[512,384]{1,0:T(8,128)S(1)} %copy-done.4), kind=kOutput, calls=%fused_computation.7 | convolution fusion | flops 404226048 | bytes 3407872 | tf_op jit(solution)/shard_map/dot_general | solution.py:28
  73.3 0.0 reduce-scatter.6.cloned.1.call-update
  73.3 0.0 reduce-scatter.4.cloned.1.call-start
  73.4 2.9 %fusion = bf16[1,1024,384]{2,1,0:T(8,128)(2,1)} fusion(bf16[512,1024]{1,0:T(8,128)(2,1)S(1)} %bitcast.28, f32[512,384]{1,0:T(8,128)S(1)} %copy-done.5, f32[512,384]{1,0:T(8,128)} %copy-done.8, f32[512,384]{1,0:T(8,128)S(1)} %copy-done.7), kind=kOutput, calls=%fused_computation.6 | convolution fusion | flops 405012480 | bytes 4194304 | tf_op jit(solution)/shard_map/dot_general | solution.py:28
  76.3 0.0 reduce-scatter.4.cloned.1.call-update
  76.3 22.9 %reduce-scatter.8.cloned.1.call-done = bf16[1,96,1024]{2,1,0:T(8,128)(2,1)} async-done(((bf16[1,384,1024]{2,1,0:T(8,128)(2,1)}), bf16[1,96,1024]{2,1,0:T(8,128)(2,1)}) %reduce-scatter.8.cloned.1.call-update) | async-done | bytes 196624 | tf_op jit(solution)/shard_map/reduce_scatter | solution.py:89
  99.2 29.7 %reduce-scatter.6.cloned.1.call-done = bf16[1,256,384]{2,1,0:T(8,128)(2,1)} async-done(((bf16[1,1024,384]{2,1,0:T(8,128)(2,1)}), bf16[1,256,384]{2,1,0:T(8,128)(2,1)}) %reduce-scatter.6.cloned.1.call-update) | async-done | bytes 196624 | tf_op jit(solution)/shard_map/reduce_scatter | solution.py:86
  128.8 29.6 %reduce-scatter.4.cloned.1.call-done = bf16[1,256,384]{2,1,0:T(8,128)(2,1)} async-done(((bf16[1,1024,384]{2,1,0:T(8,128)(2,1)}), bf16[1,256,384]{2,1,0:T(8,128)(2,1)}) %reduce-scatter.4.cloned.1.call-update) | async-done | bytes 196624 | tf_op jit(solution)/shard_map/reduce_scatter | solution.py:83
  (32 shorter events, 0.2 us)
Async XLA Ops:
  7.2 57.3 %copy-start = (bf16[1,1024,384]{2,1,0:T(8,128)(2,1)S(1)}, bf16[1,1024,384]{2,1,0:T(8,128)(2,1)}, u32[]{:S(2)}) copy-start(bf16[1,1024,384]{2,1,0:T(8,128)(2,1)} %param.11) | copy-start | bytes 2359300
  12.0 9.6 %copy-start.9 = (bf16[128,1024]{1,0:T(8,128)(2,1)S(1)}, bf16[128,1024]{1,0:T(8,128)(2,1)}, u32[]{:S(2)}) copy-start(bf16[128,1024]{1,0:T(8,128)(2,1)} %param.8) | copy-start | bytes 786436
  15.1 49.3 %all-to-all-start = ((bf16[8,64,1024]{2,1,0:T(8,128)(2,1)}), bf16[8,64,1024]{2,1,0:T(8,128)(2,1)S(1)}, u32[]{:S(2)}, u32[]{:S(2)}) async-start(bf16[8,64,1024]{2,1,0:T(8,128)(2,1)} %bitcast), calls=%async_computation | async-start | bytes 2097152 | tf_op jit(solution)/shard_map/all_to_all | solution.py:62
  21.5 77.7 %reduce-scatter.8.cloned.1.call-start = ((), (), s32[]{:S(2)}) async-start(), calls=%async_computation.6 | async-start | bytes 983040 | tf_op jit(solution)/shard_map/reduce_scatter | solution.py:89
  23.5 2.7 %copy-start.10 = (f32[128,3]{0,1:T(4,128)S(1)}, f32[128,3]{0,1:T(4,128)}, u32[]{:S(2)}) copy-start(f32[128,3]{0,1:T(4,128)} %param.10) | copy-start | bytes 4612
  29.7 1.2 copy-start.1
  31.0 4.9 %collective-permute-start = (bf16[1,64,1024]{2,1,0:T(8,128)(2,1)S(1)}, bf16[1,64,1024]{2,1,0:T(8,128)(2,1)S(1)}, u32[]{:S(2)}, u32[]{:S(2)}) collective-permute-start(bf16[1,64,1024]{2,1,0:T(8,128)(2,1)S(1)} %get-tuple-element.9), channel_id=1, source_target_pairs={{0,4},{4,0},{8,12},{12,8},{16,20},{20,16},{24,28},{28,24},{1,5},{5... | collective-permute-start | bytes 393224 | tf_op jit(solution)/shard_map/ppermute | solution.py:19
  31.5 10.9 %collective-permute-start.1 = (bf16[1,64,1024]{2,1,0:T(8,128)(2,1)S(1)}, bf16[1,64,1024]{2,1,0:T(8,128)(2,1)S(1)}, u32[]{:S(2)}, u32[]{:S(2)}) collective-permute-start(bf16[1,64,1024]{2,1,0:T(8,128)(2,1)S(1)} %get-tuple-element.8), channel_id=1, source_target_pairs={{0,8},{4,12},{8,0},{12,4},{16,24},{20,28},{24,16},{28,20},{1,9},{5... | collective-permute-start | bytes 393224 | tf_op jit(solution)/shard_map/ppermute | solution.py:19
  33.2 12.1 %collective-permute-start.2 = (bf16[1,64,1024]{2,1,0:T(8,128)(2,1)S(1)}, bf16[1,64,1024]{2,1,0:T(8,128)(2,1)S(1)}, u32[]{:S(2)}, u32[]{:S(2)}) collective-permute-start(bf16[1,64,1024]{2,1,0:T(8,128)(2,1)S(1)} %get-tuple-element.7), channel_id=1, source_target_pairs={{0,12},{4,8},{8,4},{12,0},{16,28},{20,24},{24,20},{28,16},{1,13},{... | collective-permute-start | bytes 393224 | tf_op jit(solution)/shard_map/ppermute | solution.py:19
  33.2 29.5 %collective-permute-start.3 = (bf16[1,64,1024]{2,1,0:T(8,128)(2,1)S(1)}, bf16[1,64,1024]{2,1,0:T(8,128)(2,1)S(1)}, u32[]{:S(2)}, u32[]{:S(2)}) collective-permute-start(bf16[1,64,1024]{2,1,0:T(8,128)(2,1)S(1)} %get-tuple-element.6), channel_id=1, source_target_pairs={{0,16},{4,20},{8,24},{12,28},{16,0},{20,4},{24,8},{28,12},{1,17},{... | collective-permute-start | bytes 393224 | tf_op jit(solution)/shard_map/ppermute | solution.py:19
  35.8 28.5 %collective-permute-start.4 = (bf16[1,64,1024]{2,1,0:T(8,128)(2,1)S(1)}, bf16[1,64,1024]{2,1,0:T(8,128)(2,1)S(1)}, u32[]{:S(2)}, u32[]{:S(2)}) collective-permute-start(bf16[1,64,1024]{2,1,0:T(8,128)(2,1)S(1)} %get-tuple-element.5), channel_id=1, source_target_pairs={{0,20},{4,16},{8,28},{12,24},{16,4},{20,0},{24,12},{28,8},{1,21},{... | collective-permute-start | bytes 393224 | tf_op jit(solution)/shard_map/ppermute | solution.py:19
  35.9 28.4 %collective-permute-start.5 = (bf16[1,64,1024]{2,1,0:T(8,128)(2,1)S(1)}, bf16[1,64,1024]{2,1,0:T(8,128)(2,1)S(1)}, u32[]{:S(2)}, u32[]{:S(2)}) collective-permute-start(bf16[1,64,1024]{2,1,0:T(8,128)(2,1)S(1)} %get-tuple-element.4), channel_id=1, source_target_pairs={{0,24},{4,28},{8,16},{12,20},{16,8},{20,12},{24,0},{28,4},{1,25},{... | collective-permute-start | bytes 393224 | tf_op jit(solution)/shard_map/ppermute | solution.py:19
  42.5 21.9 %collective-permute-start.6 = (bf16[1,64,1024]{2,1,0:T(8,128)(2,1)S(1)}, bf16[1,64,1024]{2,1,0:T(8,128)(2,1)S(1)}, u32[]{:S(2)}, u32[]{:S(2)}) collective-permute-start(bf16[1,64,1024]{2,1,0:T(8,128)(2,1)S(1)} %get-tuple-element.3), channel_id=1, source_target_pairs={{0,28},{4,24},{8,20},{12,16},{16,12},{20,8},{24,4},{28,0},{1,29},{... | collective-permute-start | bytes 393224 | tf_op jit(solution)/shard_map/ppermute | solution.py:19
  64.4 1.1 copy-start.2
  65.6 0.9 copy-start.3
  66.3 0.9 copy-start.6
  68.7 60.1 %reduce-scatter.6.cloned.1.call-start = ((), (), s32[]{:S(2)}) async-start(), calls=%async_computation.5 | async-start | bytes 983040 | tf_op jit(solution)/shard_map/reduce_scatter | solution.py:86
  68.7 2.8 %copy-start.4 = (f32[512,384]{1,0:T(8,128)S(1)}, f32[512,384]{1,0:T(8,128)}, u32[]{:S(2)}) copy-start(f32[512,384]{1,0:T(8,128)} %copy-done.3) | copy-start | bytes 2359300
  70.7 0.9 copy-start.8
  71.6 1.8 %copy-start.5 = (f32[512,384]{1,0:T(8,128)S(1)}, f32[512,384]{1,0:T(8,128)}, u32[]{:S(2)}) copy-start(f32[512,384]{1,0:T(8,128)} %copy-done.3) | copy-start | bytes 2359300
  71.6 1.8 %copy-start.7 = (f32[512,384]{1,0:T(8,128)S(1)}, f32[512,384]{1,0:T(8,128)}, u32[]{:S(2)}) copy-start(f32[512,384]{1,0:T(8,128)} %copy-done.6) | copy-start | bytes 2359300
  73.3 85.2 %reduce-scatter.4.cloned.1.call-start = ((), (), s32[]{:S(2)}) async-start(), calls=%async_computation.4 | async-start | bytes 983040 | tf_op jit(solution)/shard_map/reduce_scatter | solution.py:83
Sparse Core Ops, SparseCore 0:
  68.8 30.3 reduce-scatter.7
  102.6 26.1 reduce-scatter.5
  132.3 26.1 reduce-scatter.3
